TPU v7x, 32 devices: a whole 2x2x4 slice. The times are simulated.
32 devices in a mesh: row: 8 (over z, core), rep: 4 (over y, x).
Axes of the slice: x: 2, y: 2, z: 4, core: 2. Of those that a mesh axis runs over, the one named last changes fastest.
Arguments:
- features: bfloat16 [4096, 256], P(('row', 'rep')), may hold values from -6 to 6
- weight: bfloat16 [256, 256], replicated, may hold values from -0.375 to 0.375
- cotangent: bfloat16 [4096, 256], P(('row', 'rep')), may hold values from -6 to 6
- adjacency: bfloat16 [8, 4, 24, 128, 128], P('row', 'rep'), may hold values from -0.15625 to 0.15625
- tile_out: int32 [8, 4, 24], P('row', 'rep'), may hold values from 0 to 3
- tile_in: int32 [8, 4, 24], P('row', 'rep'), may hold values from 0 to 7
- live_count: int32 [8, 4], P('row', 'rep'), may hold values from 6 to 24, as said below
Outputs:
- activated: bfloat16 [4096, 256], P(('row', 'rep'))
- weight_grad: float32 [256, 256], replicated
- feature_grad: float32 [4096, 256], P(('row', 'rep'))
Inputs may be any that keep to these rules, and one draw needn't show every extreme that they name: `live_count`: live tile slots of one device; some device has all 24 slots live in every draw.
All inputs are finite; a program needn't handle non-finite values.
Results may differ from a plain program's by a relative error of at most 0.02.
Values may be sent and summed in bfloat16 or wider, within the bound.
A program may use at most 64 MiB of HBM per device.

v0:
```python
import functools
import math

import jax
import jax.numpy as jnp
from jax import lax
from jax.experimental import pallas as pl
from jax.experimental.pallas import tpu as pltpu
from jax.sharding import PartitionSpec as P

MESH = pl.DeviceIdType.MESH
F32 = jnp.float32
BF16 = jnp.bfloat16


def each(first, last, step):
    if last - first <= 4:
        for index in range(first, last):
            step(index)
    else:
        lax.fori_loop(first, last, lambda index, unused: (step(index), unused)[1], 0)


def dot(left, right):
    return jnp.dot(left, right, preferred_element_type=F32)


def kernel(
    Z, C, S,
    feat_hbm, weight_hbm, cot_hbm, adj_hbm, tout_hbm, tin_hbm, live_ref,
    act_ref, wgrad_ref, fgrad_ref,
    tiles, cum, fwd_adj, bwd_adj, feat, weight_ref, cot_ref,
    acc, own_part, part_send, part_recv, grads,
    pair_send, pair_recv, ret_send, ret_recv,
    w_part, w_pair_send, w_pair_recv, w_half, w_rep_send, w_rep_recv, w_z, w_all,
    tout_ref, tin_ref, pos,
    local_sem, feat_send_sem, feat_fwd_sem, feat_recv_sem,
    part_send_sem, part_recv_sem, grad_send_sem, grad_recv_sem,
    pair_send_sem, pair_recv_sem, ret_send_sem, ret_recv_sem,
    w_pair_sem, w_rep_send_sem, w_rep_recv_sem, w_z_send_sem, w_z_recv_sem,
    w_gather_send_sem, w_gather_recv_sem,
):
    r = lax.axis_index("row")
    c = lax.axis_index("rep")
    z = r // 2
    k = r % 2
    pr = 2 * z + 1 - k
    B = tiles.shape[1]
    W = feat.shape[3]
    halves = feat.shape[0]

    def cols(h):
        return slice(h * W, (h + 1) * W)

    def z_at(d):
        return (z + d) % Z

    def z_from(d):
        return (z + Z - d) % Z

    def c_at(e):
        return (c + e) % C

    def c_from(e):
        return (c + C - e) % C

    def remote(src, dst, send_sem, recv_sem, **where):
        return pltpu.make_async_remote_copy(
            src_ref=src, dst_ref=dst, send_sem=send_sem, recv_sem=recv_sem,
            device_id=where, device_id_type=MESH,
        )

    def to_partner(src, dst, send_sem, recv_sem):
        return remote(src, dst, send_sem, recv_sem, row=pr)

    barrier = pltpu.get_barrier_semaphore()

    def greet(**where):
        pl.semaphore_signal(barrier, inc=1, device_id=where, device_id_type=MESH)

    each(1, Z, lambda d: greet(row=2 * z_at(d) + k))
    each(1, C, lambda e: greet(rep=c_at(e)))
    greet(row=pr)
    each(1, C, lambda e: greet(row=pr, rep=c_at(e)))

    own_copies = [
        pltpu.make_async_copy(feat_hbm.at[:, cols(h)], feat.at[h, r], local_sem.at[6 + h])
        for h in range(halves)
    ]
    tile_copy = pltpu.make_async_copy(adj_hbm.at[0, 0], tiles, local_sem.at[0])
    weight_copy = pltpu.make_async_copy(weight_hbm, weight_ref, local_sem.at[1])
    cot_copy = pltpu.make_async_copy(cot_hbm, cot_ref, local_sem.at[2])
    id_copies = [
        pltpu.make_async_copy(tout_hbm, tout_ref, local_sem.at[3]),
        pltpu.make_async_copy(tin_hbm, tin_ref, local_sem.at[4]),
    ]
    for copy in id_copies + [tile_copy] + own_copies + [weight_copy, cot_copy]:
        copy.start()
    pl.semaphore_wait(barrier, 1 + (Z - 1) + 2 * (C - 1))

    def feat_send(h, d):
        return remote(
            feat_hbm.at[:, cols(h)], feat.at[h, r], feat_send_sem.at[h, d],
            feat_recv_sem.at[h, r], row=2 * z_at(d) + k,
        )

    def feat_forward(h, d):
        q = 2 * z_from(d) + k
        return to_partner(
            feat.at[h, q], feat.at[h, q], feat_fwd_sem.at[h, d], feat_recv_sem.at[h, q]
        )

    def feat_wait(h, q):
        to_partner(
            feat.at[h, q], feat.at[h, q], feat_fwd_sem.at[h, 0], feat_recv_sem.at[h, q]
        ).wait_recv()

    feat_pairs = [
        to_partner(
            feat_hbm.at[:, cols(h)], feat.at[h, r], feat_fwd_sem.at[h, 0], feat_recv_sem.at[h, r]
        )
        for h in range(halves)
    ]
    for h in range(halves):
        each(1, Z, lambda d: feat_send(h, d).start())
        feat_pairs[h].start()

    for copy in id_copies:
        copy.wait()
    live = live_ref[0, 0]
    for s in range(S):
        pos[s] = jnp.where(s < live, tin_ref[0, 0, s] * C + tout_ref[0, 0, s], -1)
    tile_copy.wait()
    cum[S] = jnp.zeros((B, B), F32)
    for s in range(S):
        prev = jnp.int32(S)
        for other in range(s):
            prev = jnp.where(pos[other] == pos[s], other, prev)
        term = tiles[s].astype(F32)
        cum[s] = term + cum[prev] if s else term

    def place(zz, unused):
        for kk in range(2):
            for b in range(C):
                spot = (2 * zz + kk) * C + b
                last = jnp.int32(S)
                for s in range(S):
                    last = jnp.where(pos[s] == spot, s, last)
                block = cum[last]
                fwd_adj[zz, b * B:(b + 1) * B, kk * B:(kk + 1) * B] = block.astype(BF16)
                bwd_adj[2 * zz + kk, :, b * B:(b + 1) * B] = block.T.astype(BF16)
        return unused

    lax.fori_loop(0, Z, place, 0)

    def pair_feats(h, zz):
        return feat[h, pl.ds(2 * zz, 2)].reshape(2 * B, W)

    def part_copy(h, e):
        return remote(
            part_send.at[h, e], part_recv.at[h, c], part_send_sem.at[h, e],
            part_recv_sem.at[h, c], rep=c_at(e),
        )

    end = z_from(Z - 1)
    for h in range(halves):
        own_copies[h].wait()
        feat_wait(h, pr)
        acc[...] = dot(fwd_adj[z], pair_feats(h, z))

        def take(d):
            feat_wait(h, 2 * z_from(d) + k)
            feat_forward(h, d).start()

        def add_chip(d):
            take(d + 1)
            zz = z_from(d)
            feat_wait(h, 2 * zz + 1 - k)
            acc[...] += dot(fwd_adj[zz], pair_feats(h, zz))

        take(1)
        each(1, Z - 1, add_chip)
        feat_wait(h, 2 * end + 1 - k)

        def part_of(b):
            rows = pl.ds(pl.multiple_of(b * B, B), B)
            return acc[rows] + dot(fwd_adj[end, rows], pair_feats(h, end))

        def send_part(e):
            part_send[h, e] = part_of(c_at(e)).astype(BF16)
            part_copy(h, e).start()

        each(1, C, send_part)
        own_part[h] = part_of(c)

    weight_copy.wait()
    cot_copy.wait()
    weight = weight_ref[...]
    pre = None
    agg_halves = []
    for h in range(halves):

        def add_part(e):
            src = c_from(e)
            remote(
                part_send.at[h, e], part_recv.at[h, src], part_send_sem.at[h, e],
                part_recv_sem.at[h, src], rep=c_at(e),
            ).wait_recv()
            own_part[h] += part_recv[h, src].astype(F32)

        each(1, C, add_part)
        agg_half = own_part[h].astype(BF16)
        agg_halves.append(agg_half)
        term = dot(agg_half, weight[cols(h)])
        pre = term if pre is None else pre + term

    sig = jax.nn.sigmoid(pre)
    grad_pre = (cot_ref[...].astype(F32) * sig * (1.0 + pre * (1.0 - sig))).astype(BF16)

    def grad_copy(h, e):
        return remote(
            grads.at[h, c], grads.at[h, c], grad_send_sem.at[h, e], grad_recv_sem.at[h, c],
            rep=c_at(e),
        )

    def make_grads(h):
        grads[h, c] = lax.dot_general(
            grad_pre, weight[cols(h)], (((1,), (1,)), ((), ())), preferred_element_type=F32
        ).astype(BF16)

    def send_grads(h):
        each(1, C, lambda e: grad_copy(h, e).start())

    def grad_wait(h):
        def one(e):
            src = c_from(e)
            remote(
                grads.at[h, src], grads.at[h, src], grad_send_sem.at[h, e],
                grad_recv_sem.at[h, src], rep=c_at(e),
            ).wait_recv()

        each(1, C, one)

    make_grads(0)
    send_grads(0)

    agg = jnp.concatenate(agg_halves, axis=1)
    w_part[...] = lax.dot_general(
        agg, grad_pre, (((0,), (0,)), ((), ())), preferred_element_type=F32
    ).reshape(w_part.shape)
    w_pair_send[...] = w_part[1 - k].astype(BF16)
    w_pair = to_partner(w_pair_send, w_pair_recv, w_pair_sem.at[0], w_pair_sem.at[1])
    w_pair.start()
    for h in range(1, halves):
        make_grads(h)
    act_ref[...] = (pre * sig).astype(BF16)
    w_pair.wait_recv()
    w_half[...] = w_part[k] + w_pair_recv[...].astype(F32)
    w_rep_send[...] = w_half[...].astype(BF16)

    def w_rep_copy(e):
        dst = c_at(e)
        return remote(
            w_rep_send.at[dst], w_rep_recv.at[c], w_rep_send_sem.at[e], w_rep_recv_sem.at[c],
            rep=dst,
        )

    each(1, C, lambda e: w_rep_copy(e).start())
    for h in range(1, halves):
        send_grads(h)

    def returned(h, q):
        return dot(bwd_adj[q], grads[h].reshape(C * B, W))

    def pair_copy(h, j):
        zz = z_at(j)
        return to_partner(
            pair_send.at[h, zz], pair_recv.at[h, zz], pair_send_sem.at[h, zz],
            pair_recv_sem.at[h, zz],
        )

    def ret_copy(h, d):
        return remote(
            ret_send.at[h, d], ret_recv.at[h, z], ret_send_sem.at[h, d], ret_recv_sem.at[h, z],
            row=2 * z_at(d) + k,
        )

    def w_z_copy(d):
        return remote(
            w_z.at[z], w_z.at[z], w_z_send_sem.at[d], w_z_recv_sem.at[z], row=2 * z_at(d) + k
        )

    def return_half(h):
        def send_pair(j):
            zz = z_at(j)
            pair_send[h, zz] = returned(h, 2 * zz + 1 - k).astype(BF16)
            pair_copy(h, j).start()

        def joined(j):
            zz = z_at(j)
            value = returned(h, 2 * zz + k)
            pair_copy(h, j).wait_recv()
            return value + pair_recv[h, zz].astype(F32)

        def send_ret(d):
            ret_send[h, d] = joined(d).astype(BF16)
            ret_copy(h, d).start()

        grad_wait(h)
        each(1, Z + 1, send_pair)
        each(1, Z, send_ret)
        fgrad_ref[:, cols(h)] = joined(Z)

    def add_w_rep(e):
        src = c_from(e)
        remote(
            w_rep_send.at[src], w_rep_recv.at[src], w_rep_send_sem.at[e], w_rep_recv_sem.at[src],
            rep=src,
        ).wait_recv()
        w_half[c] += w_rep_recv[src].astype(F32)

    each(1, C, add_w_rep)
    w_z[z] = w_half[c].astype(BF16)
    each(1, Z, lambda d: w_z_copy(d).start())
    return_half(0)
    for h in range(1, halves):
        return_half(h)

    def w_z_wait(d):
        src = z_from(d)
        remote(
            w_z.at[src], w_z.at[src], w_z_send_sem.at[d], w_z_recv_sem.at[src],
            row=2 * src + k,
        ).wait_recv()

    each(1, Z, w_z_wait)
    w_all[k, c] = jnp.sum(w_z[...].astype(F32), axis=0).astype(BF16)

    def w_gather_copy(kk, e):
        return remote(
            w_all.at[k, c], w_all.at[k, c], w_gather_send_sem.at[kk, e],
            w_gather_recv_sem.at[k, c], row=2 * z + (k + kk) % 2, rep=c_at(e),
        )

    def w_gather_wait(kk, e):
        src_k, src_c = (k + kk) % 2, c_from(e)
        remote(
            w_all.at[src_k, src_c], w_all.at[src_k, src_c], w_gather_send_sem.at[kk, e],
            w_gather_recv_sem.at[src_k, src_c], row=2 * z + src_k, rep=src_c,
        ).wait_recv()

    for kk in range(2):
        each(1 - kk, C, lambda e: w_gather_copy(kk, e).start())

    def add_ret(h, d):
        src = z_from(d)
        remote(
            ret_send.at[h, d], ret_recv.at[h, src], ret_send_sem.at[h, d],
            ret_recv_sem.at[h, src], row=2 * src + k,
        ).wait_recv()
        fgrad_ref[:, cols(h)] += ret_recv[h, src].astype(F32)

    for h in range(halves):
        each(1, Z, lambda d: add_ret(h, d))
    for kk in range(2):
        each(1 - kk, C, lambda e: w_gather_wait(kk, e))
    wgrad_ref[...] = w_all[...].astype(F32).reshape(wgrad_ref.shape)

    w_pair.wait_send()
    each(1, Z, lambda d: w_z_copy(d).wait_send())
    for h in range(halves):
        feat_pairs[h].wait_send()
        pair_copy(h, Z).wait_send()

        def drain_z(d):
            feat_send(h, d).wait_send()
            feat_forward(h, d).wait_send()
            pair_copy(h, d).wait_send()
            ret_copy(h, d).wait_send()

        def drain_c(e):
            part_copy(h, e).wait_send()
            grad_copy(h, e).wait_send()

        each(1, Z, drain_z)
        each(1, C, drain_c)

    each(1, C, lambda e: w_rep_copy(e).wait_send())
    for kk in range(2):
        each(1 - kk, C, lambda e: w_gather_copy(kk, e).wait_send())


def write_out(*refs):
    count = len(refs) // 2
    sem = refs[-1]
    copies = [
        pltpu.make_async_copy(refs[i], refs[count + i], sem.at[i]) for i in range(count)
    ]
    for copy in copies:
        copy.start()
    for copy in copies:
        copy.wait()


def solution(mesh):
    R = mesh.shape["row"]
    C = mesh.shape["rep"]
    Z = R // 2

    def body(features, weight, cotangent, adjacency, tile_out, tile_in, live_count):
        B, F = features.shape
        S = adjacency.shape[2]
        H = F // (2 * C)
        N = 2
        W = F // N
        anywhere = pl.BlockSpec(memory_space=pl.ANY)
        vector = pl.BlockSpec(memory_space=pltpu.VMEM)
        dma = pltpu.SemaphoreType.DMA
        out_shape = (
            jax.ShapeDtypeStruct((B, F), BF16),
            jax.ShapeDtypeStruct(weight.shape, F32),
            jax.ShapeDtypeStruct((B, F), F32),
        )
        buffers = [
            ((S, B, B), BF16), ((S + 1, B, B), F32),
            ((Z, C * B, 2 * B), BF16), ((R, B, C * B), BF16),
            ((N, R, B, W), BF16), (weight.shape, BF16), ((B, F), BF16),
            ((C * B, W), F32), ((N, B, W), F32),
            ((N, C, B, W), BF16), ((N, C, B, W), BF16), ((N, C, B, W), BF16),
            ((N, Z, B, W), BF16), ((N, Z, B, W), BF16),
            ((N, Z, B, W), BF16), ((N, Z, B, W), BF16),
            ((2, C, H, F), F32), ((C, H, F), BF16), ((C, H, F), BF16), ((C, H, F), F32),
            ((C, H, F), BF16), ((C, H, F), BF16), ((Z, H, F), BF16), ((2, C, H, F), BF16),
        ]
        held = sum(math.prod(shape) * (4 if kind == F32 else 2) for shape, kind in buffers)
        results = pl.pallas_call(
            functools.partial(kernel, Z, C, S),
            out_shape=out_shape,
            in_specs=[pl.BlockSpec(memory_space=pltpu.HBM)] * 6
            + [pl.BlockSpec(memory_space=pltpu.SMEM)],
            out_specs=(vector, vector, vector),
            scratch_shapes=[pltpu.VMEM(shape, kind) for shape, kind in buffers] + [
                pltpu.SMEM(tile_out.shape, jnp.int32),
                pltpu.SMEM(tile_in.shape, jnp.int32),
                pltpu.SMEM((S,), jnp.int32),
                dma((6 + N,)), dma((N, Z)), dma((N, Z)), dma((N, R)),
                dma((N, C)), dma((N, C)), dma((N, C)), dma((N, C)),
                dma((N, Z)), dma((N, Z)), dma((N, Z)), dma((N, Z)),
                dma((2,)), dma((C,)), dma((C,)), dma((Z,)), dma((Z,)),
                dma((2, C)), dma((2, C)),
            ],
            compiler_params=pltpu.CompilerParams(
                collective_id=0, has_side_effects=True,
                vmem_limit_bytes=min(held + 8 * 2 ** 20, 60 * 2 ** 20),
            ),
        )(*(
            pltpu.with_memory_space_constraint(arg, pltpu.HBM)
            for arg in (features, weight, cotangent, adjacency, tile_out, tile_in)
        ), live_count)
        return pl.pallas_call(
            write_out,
            out_shape=out_shape,
            in_specs=[vector] * 3,
            out_specs=(anywhere,) * 3,
            scratch_shapes=[dma((3,))],
            compiler_params=pltpu.CompilerParams(vmem_limit_bytes=4 * 2 ** 20),
        )(*results)

    return jax.shard_map(
        body,
        mesh=mesh,
        in_specs=(
            P(("row", "rep"), None),
            P(),
            P(("row", "rep"), None),
            P("row", "rep", None, None, None),
            P("row", "rep", None),
            P("row", "rep", None),
            P("row", "rep"),
        ),
        out_specs=(P(("row", "rep"), None), P(), P(("row", "rep"), None)),
        check_vma=False,
    )
```

profile of v0, /device:TPU:0, one launch (start us, length us, event | category | flops | bytes accessed | tf_op | source)
XLA Modules:
  0.0 36.3 jit_solution(15594041560738473587)
XLA Ops:
  1.3 34.2 %shard_map.94 = (bf16[128,256]{1,0:T(8,128)(2,1)S(1)}, f32[256,256]{1,0:T(8,128)S(1)}, f32[128,256]{1,0:T(8,128)S(1)}) custom-call(bf16[128,256]{1,0:T(8,128)(2,1)} %feat_hbm.1, bf16[256,256]{1,0:T(8,128)(2,1)} %weight_hbm.1, bf16[128,256]{1,0:T(8,128)(2,1)} %cot_hbm.1, bf16[1,1,24,128,128]{4,3,2,1,0:T(8,128)(2,1)} %adj_hbm.1, s32[1,1,24]{2,1,0:T(1,128)} %tout_hbm.1, ...), custom_call_target="tpu_custom_call" | custom-call | tf_op jit(solution)/shard_map/pallas_call | solution.py:436
  35.5 0.8 %shard_map.95 = (bf16[128,256]{1,0:T(8,128)(2,1)}, f32[256,256]{1,0:T(8,128)}, f32[128,256]{1,0:T(8,128)}) custom-call(bf16[128,256]{1,0:T(8,128)(2,1)S(1)} %get-tuple-element.6.refs_0_, f32[256,256]{1,0:T(8,128)S(1)} %get-tuple-element.7.refs_1_, f32[128,256]{1,0:T(8,128)S(1)} %get-tuple-element.8.refs_2_), custom_call_target="tpu_custom_call" | custom-call | tf_op jit(solution)/shard_map/pallas_call | solution.py:460
where the time goes:
time: 36.4 us; the launch traced here: 36.3 us
  Pallas kernels  35 us (96%)
  between operations  1.29 us (4%)
    pallas_call x1, Pallas kernels, body(): pl.pallas_call(functools.partial(kernel, Z, C, S), out_shape=out_shape, i...  34.2 us
    pallas_call x1, Pallas kernels, body(): pl.pallas_call(write_out, out_shape=out_shape, in_specs=[vector] * 3, out...  0.79 us

commit v1 on v0

v1 whole, which is shorter than its diff:
```python
import functools
import math

import jax
import jax.numpy as jnp
from jax import lax
from jax.experimental import pallas as pl
from jax.experimental.pallas import tpu as pltpu
from jax.sharding import PartitionSpec as P

MESH = pl.DeviceIdType.MESH
F32 = jnp.float32
BF16 = jnp.bfloat16


def each(first, last, step):
    if last - first <= 4:
        for index in range(first, last):
            step(index)
    else:
        lax.fori_loop(first, last, lambda index, unused: (step(index), unused)[1], 0)


def dot(left, right):
    return jnp.dot(left, right, preferred_element_type=F32)


def grid_of(count):
    across = max(n for n in range(1, math.isqrt(count) + 1) if count % n == 0)
    return across, count // across


def kernel(
    Z, C, S,
    feat_hbm, weight_hbm, cot_hbm, adj_hbm, tout_hbm, tin_hbm, live_ref,
    act_ref, wgrad_ref, fgrad_ref,
    tiles, cum, fwd_adj, bwd_adj, feat, weight_ref, cot_ref,
    acc, own_part, part_send, part_recv, grads,
    pair_send, pair_recv, ret_send, ret_recv,
    w_part, w_pair_send, w_pair_recv, w_half, w_rep_send, w_rep_recv, w_z, w_all,
    tout_ref, tin_ref, pos,
    ready, token, local_sem, feat_send_sem, feat_fwd_sem, feat_recv_sem,
    part_send_sem, part_recv_sem, grad_send_sem, grad_recv_sem,
    pair_send_sem, pair_recv_sem, ret_send_sem, ret_recv_sem,
    w_pair_sem, w_rep_sem, w_z_sem, w_gather_sem,
):
    r = lax.axis_index("row")
    c = lax.axis_index("rep")
    z = r // 2
    k = r % 2
    pr = 2 * z + 1 - k
    B = tiles.shape[1]
    W = feat.shape[3]
    halves = feat.shape[0]
    CY, CX = grid_of(C)

    def cols(h):
        return slice(h * W, (h + 1) * W)

    def c_at(e):
        return (c // CX + e // CX) % CY * CX + (c % CX + e % CX) % CX

    def c_from(e):
        return (c // CX + CY - e // CX) % CY * CX + (c % CX + CX - e % CX) % CX

    def far_first(step):
        each(1, C, lambda i: step(C - i))

    def other(j):
        high = 2 * z // Z
        down = Z - j - (z + j) // Z
        up = j - 1 + (j - 1 - z + Z) // Z
        return (1 - high) * down + high * up

    far_end = (1 - 2 * z // Z) * (Z - 1)

    def remote(src, dst, send_sem, recv_sem, **where):
        return pltpu.make_async_remote_copy(
            src_ref=src, dst_ref=dst, send_sem=send_sem, recv_sem=recv_sem,
            device_id=where, device_id_type=MESH,
        )

    def to_partner(src, dst, send_sem, recv_sem):
        return remote(src, dst, send_sem, recv_sem, row=pr)

    barrier = pltpu.get_barrier_semaphore()
    near = sorted({1 % CX, CX - 1, 1 % CY * CX, (CY - 1) * CX} - {0})
    rounds = CY // 2 + CX // 2 - 1

    def greet(semaphore, **where):
        pl.semaphore_signal(semaphore, inc=1, device_id=where, device_id_type=MESH)

    def on_sides(step):
        @pl.when(z < Z - 1)
        def _():
            step(1)

        @pl.when(z > 0)
        def _():
            step(0)

    def side_row(side):
        return 2 * (z + 2 * side - 1) + k

    on_sides(lambda side: greet(barrier, row=side_row(side)))
    greet(barrier, row=pr)
    for e in near:
        greet(barrier, rep=c_at(e))

    own_copies = [
        pltpu.make_async_copy(feat_hbm.at[:, cols(h)], feat.at[h, r], local_sem.at[5])
        for h in range(halves)
    ]
    tile_copy = pltpu.make_async_copy(adj_hbm.at[0, 0], tiles, local_sem.at[0])
    weight_copy = pltpu.make_async_copy(weight_hbm, weight_ref, local_sem.at[1])
    cot_copy = pltpu.make_async_copy(cot_hbm, cot_ref, local_sem.at[2])
    id_copies = [
        pltpu.make_async_copy(tout_hbm, tout_ref, local_sem.at[3]),
        pltpu.make_async_copy(tin_hbm, tin_ref, local_sem.at[4]),
    ]
    for copy in id_copies + [tile_copy] + own_copies + [weight_copy, cot_copy]:
        copy.start()
    sides = (z + Z - 1) // Z + (2 * Z - 2 - z) // Z
    pl.semaphore_wait(barrier, 1 + sides + len(near))

    def feat_copy(h, zz):
        return remote(
            feat_hbm.at[:, cols(h)], feat.at[h, r], feat_send_sem.at[0], feat_recv_sem.at[h, r],
            row=2 * zz + k,
        )

    def feat_forward(h, zz):
        there = feat.at[h, 2 * zz + k]
        return to_partner(there, there, feat_fwd_sem.at[0], feat_recv_sem.at[h, 2 * zz + k])

    def feat_wait(h, q):
        there = feat.at[h, q]
        to_partner(there, there, feat_fwd_sem.at[0], feat_recv_sem.at[h, q]).wait_recv()

    def send_feats(h, d):
        @pl.when(z + d < Z)
        def _():
            feat_copy(h, z + d).start()

        @pl.when(z >= d)
        def _():
            feat_copy(h, z - d).start()

    def pass_token(d):
        on_sides(lambda side: greet(token.at[d], row=side_row(side)))

    def await_token(d):
        pl.semaphore_wait(token.at[d], sides)

    for h in range(halves):
        send_feats(h, 1)
        to_partner(
            feat_hbm.at[:, cols(h)], feat.at[h, r], feat_fwd_sem.at[0], feat_recv_sem.at[h, r]
        ).start()
    if Z > 2:
        pass_token(0)
    if rounds:
        for e in near:
            greet(ready.at[0], rep=c_at(e))

    for copy in id_copies:
        copy.wait()
    live = live_ref[0, 0]
    for s in range(S):
        pos[s] = jnp.where(s < live, tin_ref[0, 0, s] * C + tout_ref[0, 0, s], -1)
    tile_copy.wait()
    cum[S] = jnp.zeros((B, B), F32)
    for s in range(S):
        prev = jnp.int32(S)
        for other_s in range(s):
            prev = jnp.where(pos[other_s] == pos[s], other_s, prev)
        term = tiles[s].astype(F32)
        cum[s] = term + cum[prev] if s else term

    def send_farther(d):
        await_token(d - 2)

        @pl.when(d < Z - 1)
        def _():
            pass_token(d - 1)

        send_feats(0, d)

    each(2, Z, send_farther)
    for h in range(1, halves):
        each(2, Z, lambda d: send_feats(h, d))

    def place(zz, unused):
        for kk in range(2):
            for b in range(C):
                spot = (2 * zz + kk) * C + b
                last = jnp.int32(S)
                for s in range(S):
                    last = jnp.where(pos[s] == spot, s, last)
                block = cum[last]
                fwd_adj[zz, b * B:(b + 1) * B, kk * B:(kk + 1) * B] = block.astype(BF16)
                bwd_adj[2 * zz + kk, :, b * B:(b + 1) * B] = block.T.astype(BF16)
        return unused

    lax.fori_loop(0, Z, place, 0)

    def relay(h, j):
        zz = other(j)
        feat_wait(h, 2 * zz + k)
        feat_forward(h, zz).start()

    def pair_feats(h, zz):
        return feat[h, pl.ds(2 * zz, 2)].reshape(2 * B, W)

    def chip_term(zz):
        for h in range(halves):
            feat_wait(h, 2 * zz + 1 - k)
        both = jnp.concatenate([pair_feats(h, zz) for h in range(halves)], axis=1)
        return dot(fwd_adj[zz], both)

    def add_chip(j):
        acc[...] += chip_term(other(j))

    def relay_all(j):
        for h in range(halves):
            relay(h, j)

    each(3, Z, lambda i: relay_all(Z + 2 - i))
    pltpu.make_async_copy(feat.at[:, r], feat.at[:, r], local_sem.at[5]).wait()
    acc[...] = chip_term(z)
    for j in range(min(2, Z - 1), 0, -1):
        relay(0, j)
    each(3, Z, lambda i: add_chip(Z + 2 - i))
    for j in range(rounds):
        if j:
            for e in near:
                greet(ready.at[j], rep=c_at(e))
        pl.semaphore_wait(ready.at[j], len(near))

    def part_copy(h, e):
        return remote(
            part_send.at[h, e], part_recv.at[h, e], part_send_sem.at[0],
            part_recv_sem.at[h], rep=c_at(e),
        )

    for h in range(halves):
        if Z > 2:
            if h + 1 < halves:
                relay(h + 1, 2)
            feat_wait(h, 2 * other(2) + 1 - k)
            acc[:, cols(h)] += dot(fwd_adj[other(2)], pair_feats(h, other(2)))
        feat_wait(h, 2 * far_end + 1 - k)

        def part_of(b):
            rows = pl.ds(pl.multiple_of(b * B, B), B)
            return acc[rows, cols(h)] + dot(fwd_adj[far_end, rows], pair_feats(h, far_end))

        def send_part(e):
            part_send[h, e] = part_of(c_at(e)).astype(BF16)
            part_copy(h, e).start()

        far_first(send_part)
        if h + 1 < halves:
            relay(h + 1, 1)
        own_part[h] = part_of(c)

    weight_copy.wait()
    cot_copy.wait()
    weight = weight_ref[...]
    pre = None
    agg_halves = []
    for h in range(halves):

        came = part_recv.at[h, pl.ds(1, C - 1)]
        remote(came, came, part_send_sem.at[0], part_recv_sem.at[h], rep=c_at(1)).wait_recv()
        total = own_part[h]
        for e in range(1, C):
            total += part_recv[h, e].astype(F32)
        agg_half = total.astype(BF16)
        agg_halves.append(agg_half)
        term = dot(agg_half, weight[cols(h)])
        pre = term if pre is None else pre + term

    sig = jax.nn.sigmoid(pre)
    grad_pre = (cot_ref[...].astype(F32) * sig * (1.0 + pre * (1.0 - sig))).astype(BF16)

    def grad_copy(h, e):
        return remote(
            grads.at[h, c], grads.at[h, c], grad_send_sem.at[0], grad_recv_sem.at[h],
            rep=c_at(e),
        )

    def make_grads(h):
        grads[h, c] = lax.dot_general(
            grad_pre, weight[cols(h)], (((1,), (1,)), ((), ())), preferred_element_type=F32
        ).astype(BF16)

    def grad_wait(h):
        came = grads.at[h, pl.ds(0, C - 1)]
        remote(came, came, grad_send_sem.at[0], grad_recv_sem.at[h], rep=c_at(1)).wait_recv()

    def send_grads(h):
        far_first(lambda e: grad_copy(h, e).start())

    make_grads(0)
    send_grads(0)

    agg = jnp.concatenate(agg_halves, axis=1)
    w_part[...] = lax.dot_general(
        agg, grad_pre, (((0,), (0,)), ((), ())), preferred_element_type=F32
    ).reshape(w_part.shape)
    w_pair_send[...] = w_part[1 - k].astype(BF16)
    w_pair = to_partner(w_pair_send, w_pair_recv, w_pair_sem.at[0], w_pair_sem.at[1])
    w_pair.start()
    for h in range(1, halves):
        make_grads(h)
    act_ref[...] = (pre * sig).astype(BF16)

    w_pair.wait_recv()
    w_half[...] = w_part[k] + w_pair_recv[...].astype(F32)
    w_rep_send[...] = w_half[...].astype(BF16)

    def w_rep_copy(e):
        return remote(
            w_rep_send.at[c_at(e)], w_rep_recv.at[e], w_rep_sem.at[0], w_rep_sem.at[1],
            rep=c_at(e),
        )

    far_first(lambda e: w_rep_copy(e).start())
    for h in range(1, halves):
        send_grads(h)

    def ends(sent, semaphore):
        remote(sent, sent, semaphore, semaphore, row=pr).wait_send()

    ends(feat.at[:, pl.ds(0, Z - 1)], feat_send_sem.at[0])
    ends(feat.at[:, pl.ds(0, Z)], feat_fwd_sem.at[0])
    ends(part_send.at[:, pl.ds(1, C - 1)], part_send_sem.at[0])

    def returned(h, q):
        return dot(bwd_adj[q], grads[h].reshape(C * B, W))

    def pair_copy(h, zz):
        return to_partner(
            pair_send.at[h, zz], pair_recv.at[h, zz], pair_send_sem.at[0],
            pair_recv_sem.at[h, zz],
        )

    def ret_copy(h, zz):
        return remote(
            ret_send.at[h, zz], ret_recv.at[h, z], ret_send_sem.at[0], ret_recv_sem.at[h],
            row=2 * zz + k,
        )

    def w_z_copy(zz):
        return remote(
            w_z.at[z], w_z.at[z], w_z_sem.at[0], w_z_sem.at[1], row=2 * zz + k
        )

    def return_half(h):
        def send_pair(zz):
            pair_send[h, zz] = returned(h, 2 * zz + 1 - k).astype(BF16)
            pair_copy(h, zz).start()

        def joined(zz):
            value = returned(h, 2 * zz + k)
            pair_copy(h, zz).wait_recv()
            return value + pair_recv[h, zz].astype(F32)

        def send_ret(j):
            zz = other(j)
            ret_send[h, zz] = joined(zz).astype(BF16)
            ret_copy(h, zz).start()

        grad_wait(h)
        each(1, Z, lambda j: send_pair(other(j)))
        send_pair(z)
        if h == 0:
            send_w_z()
        each(1, Z, send_ret)
        fgrad_ref[:, cols(h)] = joined(z)

    def send_w_z():
        came = w_rep_recv.at[pl.ds(1, C - 1)]
        remote(came, came, w_rep_sem.at[0], w_rep_sem.at[1], rep=c_at(1)).wait_recv()
        total = w_half[c]
        for e in range(1, C):
            total += w_rep_recv[e].astype(F32)
        w_z[z] = total.astype(BF16)
        each(1, Z, lambda j: w_z_copy(other(j)).start())

    for h in range(halves):
        return_half(h)

    came = w_z.at[pl.ds(0, Z - 1)]
    remote(came, came, w_z_sem.at[0], w_z_sem.at[1], row=pr).wait_recv()
    w_all[k * C + c] = jnp.sum(w_z[...].astype(F32), axis=0).astype(BF16)

    def w_gather_copy(kk, e):
        mine = w_all.at[k * C + c]
        return remote(
            mine, mine, w_gather_sem.at[0], w_gather_sem.at[1],
            row=2 * z + (k + kk) % 2, rep=c_at(e),
        )

    for kk in range(2):
        each(1 - kk, C, lambda e: w_gather_copy(kk, e).start())

    w_pair.wait_send()
    ends(grads.at[:, pl.ds(0, C - 1)], grad_send_sem.at[0])
    ends(pair_send, pair_send_sem.at[0])
    ends(w_rep_send.at[pl.ds(0, C - 1)], w_rep_sem.at[0])
    ends(w_z.at[pl.ds(0, Z - 1)], w_z_sem.at[0])
    ends(ret_send.at[:, pl.ds(0, Z - 1)], ret_send_sem.at[0])
    most = w_all.at[pl.ds(0, 2 * C - 1)]
    ends(most, w_gather_sem.at[0])

    for h in range(halves):
        came = ret_recv.at[h, pl.ds(0, Z - 1)]
        remote(came, came, ret_send_sem.at[0], ret_recv_sem.at[h], row=pr).wait_recv()
        total = fgrad_ref[:, cols(h)]
        for j in range(1, Z):
            total += ret_recv[h, other(j)].astype(F32)
        fgrad_ref[:, cols(h)] = total
    remote(most, most, w_gather_sem.at[0], w_gather_sem.at[1], row=pr).wait_recv()
    wgrad_ref[...] = w_all[...].astype(F32).reshape(wgrad_ref.shape)


def write_out(*refs):
    count = len(refs) // 2
    sem = refs[-1]
    copies = [
        pltpu.make_async_copy(refs[i], refs[count + i], sem.at[i]) for i in range(count)
    ]
    for copy in copies:
        copy.start()
    for copy in copies:
        copy.wait()


def solution(mesh):
    R = mesh.shape["row"]
    C = mesh.shape["rep"]
    Z = R // 2

    def body(features, weight, cotangent, adjacency, tile_out, tile_in, live_count):
        B, F = features.shape
        S = adjacency.shape[2]
        H = F // (2 * C)
        N = 2
        W = F // N
        CY, CX = grid_of(C)
        anywhere = pl.BlockSpec(memory_space=pl.ANY)
        vector = pl.BlockSpec(memory_space=pltpu.VMEM)
        dma = pltpu.SemaphoreType.DMA
        out_shape = (
            jax.ShapeDtypeStruct((B, F), BF16),
            jax.ShapeDtypeStruct(weight.shape, F32),
            jax.ShapeDtypeStruct((B, F), F32),
        )
        buffers = [
            ((S, B, B), BF16), ((S + 1, B, B), F32),
            ((Z, C * B, 2 * B), BF16), ((R, B, C * B), BF16),
            ((N, R, B, W), BF16), (weight.shape, BF16), ((B, F), BF16),
            ((C * B, F), F32), ((N, B, W), F32),
            ((N, C, B, W), BF16), ((N, C, B, W), BF16), ((N, C, B, W), BF16),
            ((N, Z, B, W), BF16), ((N, Z, B, W), BF16),
            ((N, Z, B, W), BF16), ((N, Z, B, W), BF16),
            ((2, C, H, F), F32), ((C, H, F), BF16), ((C, H, F), BF16), ((C, H, F), F32),
            ((C, H, F), BF16), ((C, H, F), BF16), ((Z, H, F), BF16), ((2 * C, H, F), BF16),
        ]
        held = sum(math.prod(shape) * (4 if kind == F32 else 2) for shape, kind in buffers)
        results = pl.pallas_call(
            functools.partial(kernel, Z, C, S),
            out_shape=out_shape,
            in_specs=[pl.BlockSpec(memory_space=pltpu.HBM)] * 6
            + [pl.BlockSpec(memory_space=pltpu.SMEM)],
            out_specs=(vector, vector, vector),
            scratch_shapes=[pltpu.VMEM(shape, kind) for shape, kind in buffers] + [
                pltpu.SMEM(tile_out.shape, jnp.int32),
                pltpu.SMEM(tile_in.shape, jnp.int32),
                pltpu.SMEM((S,), jnp.int32),
                pltpu.SemaphoreType.REGULAR((max(CY // 2 + CX // 2 - 1, 1),)),
                pltpu.SemaphoreType.REGULAR((max(Z - 2, 1),)),
                dma((6,)), dma((1,)), dma((1,)), dma((N, R)),
                dma((1,)), dma((N,)), dma((1,)), dma((N,)),
                dma((1,)), dma((N, Z)), dma((1,)), dma((N,)),
                dma((2,)), dma((2,)), dma((2,)), dma((2,)),
            ],
            compiler_params=pltpu.CompilerParams(
                collective_id=0, has_side_effects=True,
                vmem_limit_bytes=min(held + 8 * 2 ** 20, 60 * 2 ** 20),
            ),
        )(*(
            pltpu.with_memory_space_constraint(arg, pltpu.HBM)
            for arg in (features, weight, cotangent, adjacency, tile_out, tile_in)
        ), live_count)
        return pl.pallas_call(
            write_out,
            out_shape=out_shape,
            in_specs=[vector] * 3,
            out_specs=(anywhere,) * 3,
            scratch_shapes=[dma((3,))],
            compiler_params=pltpu.CompilerParams(vmem_limit_bytes=4 * 2 ** 20),
        )(*results)

    return jax.shard_map(
        body,
        mesh=mesh,
        in_specs=(
            P(("row", "rep"), None),
            P(),
            P(("row", "rep"), None),
            P("row", "rep", None, None, None),
            P("row", "rep", None),
            P("row", "rep", None),
            P("row", "rep"),
        ),
        out_specs=(P(("row", "rep"), None), P(), P(("row", "rep"), None)),
        check_vma=False,
    )
```

time: 36.4 us -> 33 us (0.907)
  Pallas kernels: 35 us -> 31.5 us
    pallas_call x1, Pallas kernels: 34.2 us -> 30.7 us  [body(): pl.pallas_call(functools.partial(kernel, Z, C, S), out_shape=out_shape, i...]
where the time goes in v1:
time: 33 us; the launch traced here: 32.8 us
  Pallas kernels  31.5 us (95%)
  between operations  1.29 us (4%)
    pallas_call x1, Pallas kernels, body(): pl.pallas_call(functools.partial(kernel, Z, C, S), out_shape=out_shape, i...  30.7 us
    pallas_call x1, Pallas kernels, body(): pl.pallas_call(write_out, out_shape=out_shape, in_specs=[vector] * 3, out...  0.79 us

profile of v1, /device:TPU:0, one launch (start us, length us, event | category | flops | bytes accessed | tf_op | source)
XLA Modules:
  0.0 32.8 jit_solution(5668557825789535659)
XLA Ops:
  1.3 30.7 %shard_map.94 = (bf16[128,256]{1,0:T(8,128)(2,1)S(1)}, f32[256,256]{1,0:T(8,128)S(1)}, f32[128,256]{1,0:T(8,128)S(1)}) custom-call(bf16[128,256]{1,0:T(8,128)(2,1)} %feat_hbm.1, bf16[256,256]{1,0:T(8,128)(2,1)} %weight_hbm.1, bf16[128,256]{1,0:T(8,128)(2,1)} %cot_hbm.1, bf16[1,1,24,128,128]{4,3,2,1,0:T(8,128)(2,1)} %adj_hbm.1, s32[1,1,24]{2,1,0:T(1,128)} %tout_hbm.1, ...), custom_call_target="tpu_custom_call" | custom-call | tf_op jit(solution)/shard_map/pallas_call | solution.py:473
  32.0 0.8 %shard_map.95 = (bf16[128,256]{1,0:T(8,128)(2,1)}, f32[256,256]{1,0:T(8,128)}, f32[128,256]{1,0:T(8,128)}) custom-call(bf16[128,256]{1,0:T(8,128)(2,1)S(1)} %get-tuple-element.6.refs_0_, f32[256,256]{1,0:T(8,128)S(1)} %get-tuple-element.7.refs_1_, f32[128,256]{1,0:T(8,128)S(1)} %get-tuple-element.8.refs_2_), custom_call_target="tpu_custom_call" | custom-call | tf_op jit(solution)/shard_map/pallas_call | solution.py:498

commit v2 on v1

--- a/solution.py
+++ b/solution.py
@@ -72,6 +72,14 @@
         up = j - 1 + (j - 1 - z + Z) // Z
         return (1 - high) * down + high * up
 
+    def low_first(j):
+        first = 1 - (z + Z - 1) // Z
+        up = j - 1 + (j - 1 - z + Z) // Z
+        return first * (Z - j) + (1 - first) * up
+
+    def low_rep(e):
+        return e - 1 + (e - 1 - c + C) // C
+
     far_end = (1 - 2 * z // Z) * (Z - 1)
 
     def remote(src, dst, send_sem, recv_sem, **where):
@@ -137,14 +145,31 @@
         there = feat.at[h, q]
         to_partner(there, there, feat_fwd_sem.at[0], feat_recv_sem.at[h, q]).wait_recv()
 
+    passing = Z > 3
+
     def send_feats(h, d):
-        @pl.when(z + d < Z)
+        @pl.when(z + d < Z - (passing and d == 2))
         def _():
             feat_copy(h, z + d).start()
 
-        @pl.when(z >= d)
+        @pl.when(z >= d + (passing and d == 2))
         def _():
             feat_copy(h, z - d).start()
+
+    def pass_on(h, zz):
+        there = feat.at[h, 2 * zz + k]
+        return remote(
+            there, there, feat_send_sem.at[1], feat_recv_sem.at[h, 2 * zz + k],
+            row=2 * (2 * z - zz) + k,
+        )
+
+    def at_pass(zz, step):
+        if passing:
+            @pl.when(jnp.logical_or(
+                jnp.logical_and(z == 1, zz == 2), jnp.logical_and(z == Z - 2, zz == Z - 3)
+            ))
+            def _():
+                step()
 
     def pass_token(d):
         on_sides(lambda side: greet(token.at[d], row=side_row(side)))
@@ -152,16 +177,16 @@
     def await_token(d):
         pl.semaphore_wait(token.at[d], sides)
 
+    if Z > 2:
+        pass_token(0)
+    if rounds:
+        for e in near:
+            greet(ready.at[0], rep=c_at(e))
     for h in range(halves):
         send_feats(h, 1)
         to_partner(
             feat_hbm.at[:, cols(h)], feat.at[h, r], feat_fwd_sem.at[0], feat_recv_sem.at[h, r]
         ).start()
-    if Z > 2:
-        pass_token(0)
-    if rounds:
-        for e in near:
-            greet(ready.at[0], rep=c_at(e))
 
     for copy in id_copies:
         copy.wait()
@@ -186,9 +211,8 @@
 
         send_feats(0, d)
 
-    each(2, Z, send_farther)
-    for h in range(1, halves):
-        each(2, Z, lambda d: send_feats(h, d))
+    if Z > 2:
+        send_farther(2)
 
     def place(zz, unused):
         for kk in range(2):
@@ -203,10 +227,14 @@
         return unused
 
     lax.fori_loop(0, Z, place, 0)
+    each(3, Z, send_farther)
+    for h in range(1, halves):
+        each(2, Z, lambda d: send_feats(h, d))
 
     def relay(h, j):
         zz = other(j)
         feat_wait(h, 2 * zz + k)
+        at_pass(zz, lambda: pass_on(h, zz).start())
         feat_forward(h, zz).start()
 
     def pair_feats(h, zz):
@@ -225,18 +253,43 @@
         for h in range(halves):
             relay(h, j)
 
-    each(3, Z, lambda i: relay_all(Z + 2 - i))
     pltpu.make_async_copy(feat.at[:, r], feat.at[:, r], local_sem.at[5]).wait()
     acc[...] = chip_term(z)
-    for j in range(min(2, Z - 1), 0, -1):
-        relay(0, j)
+    each(3, Z, lambda i: relay_all(Z + 2 - i))
+    far = range(1, min(2, Z - 1) + 1)
+
+    @pl.when(jnp.logical_and(z > 0, z < Z - 1))
+    def _():
+        relay_all(far[-1])
+
+    @pl.when(jnp.logical_or(z == 0, z == Z - 1))
+    def _():
+        for j in far:
+            relay(0, j)
+
     each(3, Z, lambda i: add_chip(Z + 2 - i))
+
+    @pl.when(jnp.logical_and(z > 0, z < Z - 1))
+    def _():
+        for j in far[:-1]:
+            relay_all(j)
+
+    @pl.when(jnp.logical_or(z == 0, z == Z - 1))
+    def _():
+        for h in range(1, halves):
+            for j in far:
+                relay(h, j)
+
     for j in range(rounds):
         if j:
             for e in near:
                 greet(ready.at[j], rep=c_at(e))
         pl.semaphore_wait(ready.at[j], len(near))
 
+    def part_of(h, b):
+        rows = pl.ds(pl.multiple_of(b * B, B), B)
+        return acc[rows, cols(h)] + dot(fwd_adj[far_end, rows], pair_feats(h, far_end))
+
     def part_copy(h, e):
         return remote(
             part_send.at[h, e], part_recv.at[h, e], part_send_sem.at[0],
@@ -245,24 +298,18 @@
 
     for h in range(halves):
         if Z > 2:
-            if h + 1 < halves:
-                relay(h + 1, 2)
             feat_wait(h, 2 * other(2) + 1 - k)
             acc[:, cols(h)] += dot(fwd_adj[other(2)], pair_feats(h, other(2)))
         feat_wait(h, 2 * far_end + 1 - k)
 
-        def part_of(b):
-            rows = pl.ds(pl.multiple_of(b * B, B), B)
-            return acc[rows, cols(h)] + dot(fwd_adj[far_end, rows], pair_feats(h, far_end))
-
         def send_part(e):
-            part_send[h, e] = part_of(c_at(e)).astype(BF16)
+            part_send[h, e] = part_of(h, c_at(e)).astype(BF16)
             part_copy(h, e).start()
 
         far_first(send_part)
-        if h + 1 < halves:
-            relay(h + 1, 1)
-        own_part[h] = part_of(c)
+
+    for h in range(halves):
+        own_part[h] = part_of(h, c)
 
     weight_copy.wait()
     cot_copy.wait()
@@ -333,7 +380,17 @@
     def ends(sent, semaphore):
         remote(sent, sent, semaphore, semaphore, row=pr).wait_send()
 
-    ends(feat.at[:, pl.ds(0, Z - 1)], feat_send_sem.at[0])
+    skipped = [jnp.logical_and(z == 2, passing), jnp.logical_and(z == Z - 3, passing)]
+    for count in range(3):
+        @pl.when(sum(jnp.where(one, 1, 0) for one in skipped) == count)
+        def _():
+            ends(feat.at[:, pl.ds(0, Z - 1 - count)], feat_send_sem.at[0])
+
+    for near_end in (1, Z - 2) if passing else ():
+        @pl.when(z == near_end)
+        def _():
+            ends(feat.at[:, pl.ds(0, 1)], feat_send_sem.at[1])
+
     ends(feat.at[:, pl.ds(0, Z)], feat_fwd_sem.at[0])
     ends(part_send.at[:, pl.ds(1, C - 1)], part_send_sem.at[0])
 
@@ -357,28 +414,27 @@
             w_z.at[z], w_z.at[z], w_z_sem.at[0], w_z_sem.at[1], row=2 * zz + k
         )
 
-    def return_half(h):
-        def send_pair(zz):
-            pair_send[h, zz] = returned(h, 2 * zz + 1 - k).astype(BF16)
-            pair_copy(h, zz).start()
-
-        def joined(zz):
-            value = returned(h, 2 * zz + k)
-            pair_copy(h, zz).wait_recv()
-            return value + pair_recv[h, zz].astype(F32)
-
-        def send_ret(j):
-            zz = other(j)
-            ret_send[h, zz] = joined(zz).astype(BF16)
-            ret_copy(h, zz).start()
-
+    def send_pair(h, zz):
+        pair_send[h, zz] = returned(h, 2 * zz + 1 - k).astype(BF16)
+        pair_copy(h, zz).start()
+
+    def joined(h, zz):
+        value = returned(h, 2 * zz + k)
+        pair_copy(h, zz).wait_recv()
+        return value + pair_recv[h, zz].astype(F32)
+
+    def send_ret(h, j):
+        zz = low_first(j)
+        ret_send[h, zz] = joined(h, zz).astype(BF16)
+        ret_copy(h, zz).start()
+
+    def send_pairs(h):
         grad_wait(h)
-        each(1, Z, lambda j: send_pair(other(j)))
-        send_pair(z)
-        if h == 0:
-            send_w_z()
-        each(1, Z, send_ret)
-        fgrad_ref[:, cols(h)] = joined(z)
+        each(1, Z, lambda j: send_pair(h, low_first(j)))
+        send_pair(h, z)
+
+    def own_ret(h):
+        fgrad_ref[:, cols(h)] = joined(h, z)
 
     def send_w_z():
         came = w_rep_recv.at[pl.ds(1, C - 1)]
@@ -387,24 +443,36 @@
         for e in range(1, C):
             total += w_rep_recv[e].astype(F32)
         w_z[z] = total.astype(BF16)
-        each(1, Z, lambda j: w_z_copy(other(j)).start())
-
+        each(1, Z, lambda j: w_z_copy(low_first(j)).start())
+
+    held = (Z - 1) // 3
+    send_pairs(0)
+    send_w_z()
     for h in range(halves):
-        return_half(h)
+        each(1 if h == 0 else 2, Z - held if h + 1 < halves else Z, lambda j: send_ret(h, j))
+        own_ret(h)
+        if h + 1 < halves:
+            send_pairs(h + 1)
+            send_ret(h + 1, 1)
+            each(Z - held, Z, lambda j: send_ret(h, j))
 
     came = w_z.at[pl.ds(0, Z - 1)]
     remote(came, came, w_z_sem.at[0], w_z_sem.at[1], row=pr).wait_recv()
     w_all[k * C + c] = jnp.sum(w_z[...].astype(F32), axis=0).astype(BF16)
 
-    def w_gather_copy(kk, e):
+    def w_gather_copy(other_k, dst):
         mine = w_all.at[k * C + c]
         return remote(
             mine, mine, w_gather_sem.at[0], w_gather_sem.at[1],
-            row=2 * z + (k + kk) % 2, rep=c_at(e),
-        )
-
-    for kk in range(2):
-        each(1 - kk, C, lambda e: w_gather_copy(kk, e).start())
+            row=2 * z + (k + other_k) % 2, rep=dst,
+        )
+
+    def w_gather(e):
+        for other_k in range(2):
+            w_gather_copy(other_k, low_rep(e)).start()
+
+    each(1, C, w_gather)
+    w_gather_copy(1, c).start()
 
     w_pair.wait_send()
     ends(grads.at[:, pl.ds(0, C - 1)], grad_send_sem.at[0])
@@ -482,7 +550,7 @@
                 pltpu.SMEM((S,), jnp.int32),
                 pltpu.SemaphoreType.REGULAR((max(CY // 2 + CX // 2 - 1, 1),)),
                 pltpu.SemaphoreType.REGULAR((max(Z - 2, 1),)),
-                dma((6,)), dma((1,)), dma((1,)), dma((N, R)),
+                dma((6,)), dma((2,)), dma((1,)), dma((N, R)),
                 dma((1,)), dma((N,)), dma((1,)), dma((N,)),
                 dma((1,)), dma((N, Z)), dma((1,)), dma((N,)),
                 dma((2,)), dma((2,)), dma((2,)), dma((2,)),

time: 33 us -> 32.7 us (level)
  no operation moved by 1% of the time
where the time goes in v2:
time: 32.7 us; the launch traced here: 32.6 us
  Pallas kernels  31.3 us (96%)
  between operations  1.29 us (4%)
    pallas_call x1, Pallas kernels, body(): pl.pallas_call(functools.partial(kernel, Z, C, S), out_shape=out_shape, i...  30.5 us
    pallas_call x1, Pallas kernels, body(): pl.pallas_call(write_out, out_shape=out_shape, in_specs=[vector] * 3, out...  0.79 us

profile of v2, /device:TPU:0, one launch (start us, length us, event | category | flops | bytes accessed | tf_op | source)
XLA Modules:
  0.0 32.6 jit_solution(4955308927378166152)
XLA Ops:
  1.3 30.5 %shard_map.94 = (bf16[128,256]{1,0:T(8,128)(2,1)S(1)}, f32[256,256]{1,0:T(8,128)S(1)}, f32[128,256]{1,0:T(8,128)S(1)}) custom-call(bf16[128,256]{1,0:T(8,128)(2,1)} %feat_hbm.1, bf16[256,256]{1,0:T(8,128)(2,1)} %weight_hbm.1, bf16[128,256]{1,0:T(8,128)(2,1)} %cot_hbm.1, bf16[1,1,24,128,128]{4,3,2,1,0:T(8,128)(2,1)} %adj_hbm.1, s32[1,1,24]{2,1,0:T(1,128)} %tout_hbm.1, ...), custom_call_target="tpu_custom_call" | custom-call | tf_op jit(solution)/shard_map/pallas_call | solution.py:541
  31.8 0.8 %shard_map.95 = (bf16[128,256]{1,0:T(8,128)(2,1)}, f32[256,256]{1,0:T(8,128)}, f32[128,256]{1,0:T(8,128)}) custom-call(bf16[128,256]{1,0:T(8,128)(2,1)S(1)} %get-tuple-element.6.refs_0_, f32[256,256]{1,0:T(8,128)S(1)} %get-tuple-element.7.refs_1_, f32[128,256]{1,0:T(8,128)S(1)} %get-tuple-element.8.refs_2_), custom_call_target="tpu_custom_call" | custom-call | tf_op jit(solution)/shard_map/pallas_call | solution.py:566
